TPU v7x, 512 devices: a whole 4x8x8 slice. The times are simulated.
512 devices in a mesh: row: 16 (over x_hi, y), col: 32 (over z, x_lo, core).
Axes of the slice: x: 4 (x_hi: 2, x_lo: 2; x = x_hi * 2 + x_lo), y: 8, z: 8, core: 2. Of those that a mesh axis runs over, the one named last changes fastest.
Arguments:
- operator: float32 [4096, 4096], P('row', 'col'), may hold values from -0.09375 to 0.09375
- state: float32 [4096, 4096], P('row', 'col'), may hold values from -60 to 60, as said below
- source: float32 [4096, 4096], P('row', 'col'), may hold values from -60 to 60, as said below
Outputs:
- state_next: float32 [4096, 4096], P('row', 'col')
- operator_fourth: float32 [4096, 4096], P('row', 'col')
Inputs may be any that keep to these rules, and one draw needn't show every extreme that they name: symmetric: state equals its transpose. symmetric: source equals its transpose.
All inputs are finite; a program needn't handle non-finite values.
Results may differ from a plain program's by a relative error of at most 0.000098.
Values sent between devices are 32-bit elements; how exact they have to be, the bound alone decides.
A program may use at most 64 MiB of HBM per device.

v0:
```python
import jax
import jax.numpy as jnp
from jax import lax
from jax.sharding import Mesh
from jax.sharding import PartitionSpec as P

COL = ("col_0", "col_1", "col_2")


def from_everyone(x, axis):
    copies = jnp.broadcast_to(x, (lax.axis_size(axis), *x.shape))
    return lax.all_to_all(copies, axis, split_axis=0, concat_axis=0, tiled=True)


def in_order(parts, dim):
    parts = jnp.moveaxis(parts, 0, dim)
    shape = parts.shape
    return parts.reshape(*shape[:dim], shape[dim] * shape[dim + 1], *shape[dim + 2 :])


def gather_axes(x, axes, dim):
    far, near = axes
    first = from_everyone(x, far)
    parts = jnp.swapaxes(from_everyone(first, near), 0, 1)
    return in_order(parts.reshape(-1, *x.shape), dim)


def side_by_side(arrays, axis, dim, along):
    both = jnp.concatenate(arrays, axis=along)
    whole, at, done = (lax.all_gather(both, axis, axis=dim, tiled=True), 0, [])
    for a in arrays:
        done.append(lax.slice_in_dim(whole, at, at + a.shape[along], axis=along))
        at += a.shape[along]
    return tuple(done)


def matmul(left, right):
    return jnp.dot(left, right, preferred_element_type=jnp.float32, precision=lax.Precision.HIGHEST)


def split_pieces(block, groups):
    rows, columns = block.shape
    width = columns // groups
    pieces = block.reshape(2, columns, groups, width).transpose(2, 0, 3, 1)
    return pieces.reshape(2 * groups, width, columns)


def join_pieces(pieces, groups):
    count, width, columns = pieces.shape
    joined = pieces.reshape(groups, 2, width, columns).transpose(1, 0, 2, 3)
    return joined.reshape(2 * groups * width, columns)


def folder(panel, piece):
    return matmul(panel, piece)


def on_device(operator, state, source):
    groups = lax.axis_size("row")
    row_panel = gather_axes(operator, (("col_0", "col_1"), "col_2"), 1)
    pieces = side_by_side((state, operator), "row", 0, 1)
    product = matmul(row_panel, pieces[0])
    square = matmul(row_panel, pieces[1])
    moved = lax.all_to_all(
        lax.all_to_all(
            split_pieces(product, groups), "row", split_axis=0, concat_axis=0, tiled=True
        ),
        COL,
        split_axis=0,
        concat_axis=0,
        tiled=True,
    )
    turned = join_pieces(
        lax.all_to_all(moved, "row", split_axis=0, concat_axis=0, tiled=True), groups
    )
    state_next = folder(row_panel, lax.all_gather(turned, "row", axis=0, tiled=True)) + source
    square_panel = gather_axes(square, (("col_0", "col_1"), "col_2"), 1)
    operator_fourth = folder(square_panel, lax.all_gather(square, "row", axis=0, tiled=True))
    return (state_next, operator_fourth)


def solution(mesh):
    split = Mesh(
        mesh.devices.reshape(mesh.shape["row"], 8, 2, 2), ("row", "col_0", "col_1", "col_2")
    )
    in_specs = (P("row", COL), P("row", COL), P("row", COL))
    out_specs = (P("row", COL), P("row", COL))
    return jax.shard_map(
        on_device, mesh=split, in_specs=in_specs, out_specs=out_specs, check_vma=False
    )
```

profile of v0, /device:TPU:1, one launch (start us, length us, event | category | flops | bytes accessed | tf_op | source)
XLA Modules:
  0.0 321.5 jit_solution(12370682824647606802)
XLA Ops:
  7.2 1.7 pad_maximum_fusion
  9.0 1.1 broadcast_in_dim.12
  10.1 61.1 %all_to_all.35 = f32[16,256,128]{2,1,0:T(8,128)S(1)} all-to-all(f32[16,256,128]{2,1,0:T(8,128)S(1)} %broadcast_in_dim.12), channel_id=1, replica_groups=mesh['row'=16,'col_0'=8,'col_1'=2,'col_2'=2] {'col_0','col_1'}, dimensions={0} | all-to-all | bytes 4194304 | tf_op jit(solution)/shard_map/all_to_all | solution.py:12
  71.6 9.3 %all_to_all.36 = f32[2,16,256,128]{3,2,1,0:T(8,128)S(1)} all-to-all(f32[2,16,256,128]{3,2,1,0:T(8,128)S(1)} %broadcast_in_dim.13), channel_id=1, replica_groups=mesh['row'=16,'col_0'=8,'col_1'=2,'col_2'=2] {'col_2'}, dimensions={0} | all-to-all | bytes 8388608 | tf_op jit(solution)/shard_map/all_to_all | solution.py:12
  81.0 2.4 copy.19
  83.4 5.6 %copy.20 = f32[256,32,128]{0,2,1:T(8,128)} copy(f32[256,32,128]{2,0,1:T(8,128)} %bitcast.39) | data formatting | bytes 8388608 | tf_op jit(solution)/shard_map/transpose | solution.py:16
  89.0 29.7 %all-gather.4.cloned.1.call-done = f32[4096,256]{1,0:T(8,128)} async-done(((f32[256,256]{1,0:T(8,128)}), f32[4096,256]{1,0:T(8,128)}) %all-gather.4.cloned.1.call-update) | async-done | bytes 4194320 | tf_op jit(solution)/shard_map/all_gather | solution.py:30
  118.7 7.0 %fusion.4 = f32[256,128]{0,1:T(8,128)} fusion(f32[256,4096]{0,1:T(8,128)} %bitcast.35, f32[4096,256]{1,0:T(8,128)} %all-gather.4.cloned.1.call-done), kind=kOutput, calls=%fused_computation.4 | convolution fusion | flops 1610612736 | bytes 6422528 | tf_op jit(solution)/shard_map/dot_general | solution.py:38
  125.7 6.4 %fusion.2 = f32[128,256]{1,0:T(8,128)S(1)} fusion(f32[256,4096]{0,1:T(8,128)} %bitcast.36, f32[4096,256]{1,0:T(8,128)} %all-gather.4.cloned.1.call-done), kind=kOutput, calls=%fused_computation.2 | convolution fusion | flops 1610612736 | bytes 6422528 | tf_op jit(solution)/shard_map/dot_general | solution.py:38
  132.1 13.3 %all_to_all.37 = f32[32,8,128]{2,1,0:T(8,128)S(1)} all-to-all(f32[32,8,128]{2,1,0:T(8,128)S(1)} %bitcast.41), channel_id=1, replica_groups=mesh['row'=16,'col_0'=8,'col_1'=2,'col_2'=2] {'row'}, dimensions={0} | all-to-all | bytes 262144 | tf_op jit(solution)/shard_map/all_to_all | solution.py:65
  145.5 22.9 %all_to_all.38 = f32[32,8,128]{2,1,0:T(8,128)} all-to-all(f32[32,8,128]{2,1,0:T(8,128)S(1)} %all_to_all.37), channel_id=1, replica_groups=mesh['row'=16,'col_0'=8,'col_1'=2,'col_2'=2] {'col_0','col_1','col_2'}, dimensions={0} | all-to-all | bytes 262144 | tf_op jit(solution)/shard_map/all_to_all | solution.py:64
  168.4 4.1 %all-to-all-start.4 = ((f32[32,8,128]{2,1,0:T(8,128)}), f32[32,8,128]{2,1,0:T(8,128)S(1)}, u32[]{:S(2)}, u32[]{:S(2)}) async-start(f32[32,8,128]{2,1,0:T(8,128)} %all_to_all.38), calls=%async_computation.4 | async-start | bytes 262144 | tf_op jit(solution)/shard_map/all_to_all | solution.py:74
  172.5 8.8 %all-to-all-done.4 = f32[32,8,128]{2,1,0:T(8,128)S(1)} async-done(((f32[32,8,128]{2,1,0:T(8,128)}), f32[32,8,128]{2,1,0:T(8,128)S(1)}, u32[]{:S(2)}, u32[]{:S(2)}) %all-to-all-start.4) | async-done | bytes 131104 | tf_op jit(solution)/shard_map/all_to_all | solution.py:74
  181.4 1.5 broadcast_in_dim.14
  182.9 3.7 %all-to-all-start.5 = ((f32[16,256,128]{2,1,0:T(8,128)}), f32[16,256,128]{2,1,0:T(8,128)S(1)}, u32[]{:S(2)}, u32[]{:S(2)}) async-start(f32[16,256,128]{2,1,0:T(8,128)} %broadcast_in_dim.14), calls=%async_computation.5 | async-start | bytes 4194304 | tf_op jit(solution)/shard_map/all_to_all | solution.py:12
  186.7 0.7 copy.21
  187.5 47.3 %all-to-all-done.5 = f32[16,256,128]{2,1,0:T(8,128)S(1)} async-done(((f32[16,256,128]{2,1,0:T(8,128)}), f32[16,256,128]{2,1,0:T(8,128)S(1)}, u32[]{:S(2)}, u32[]{:S(2)}) %all-to-all-start.5) | async-done | bytes 2097184 | tf_op jit(solution)/shard_map/all_to_all | solution.py:12
  235.3 10.1 %all_to_all.39 = f32[2,16,256,128]{3,2,1,0:T(8,128)S(1)} all-to-all(f32[2,16,256,128]{3,2,1,0:T(8,128)S(1)} %broadcast_in_dim.15), channel_id=1, replica_groups=mesh['row'=16,'col_0'=8,'col_1'=2,'col_2'=2] {'col_2'}, dimensions={0} | all-to-all | bytes 8388608 | tf_op jit(solution)/shard_map/all_to_all | solution.py:12
  245.4 2.4 copy.24
  247.8 5.7 %copy.25 = f32[256,32,128]{0,2,1:T(8,128)} copy(f32[256,32,128]{2,0,1:T(8,128)} %bitcast.40) | data formatting | bytes 8388608 | tf_op jit(solution)/shard_map/transpose | solution.py:16
  253.5 10.2 %fusion.8 = f32[256,128]{1,0:T(8,128)} fusion(f32[256,4096]{0,1:T(8,128)} %bitcast.38, f32[4096,128]{0,1:T(8,128)} %all-gather.8.cloned.1.call-done), kind=kOutput, calls=%fused_computation.8 | convolution fusion | flops 1610612736 | bytes 6422528 | tf_op jit(solution)/shard_map/dot_general | solution.py:38
  263.7 44.2 %all-gather.6.cloned.1.call-done = f32[4096,128]{1,0:T(8,128)} async-done(((f32[256,128]{1,0:T(8,128)}), f32[4096,128]{1,0:T(8,128)}) %all-gather.6.cloned.1.call-update) | async-done | bytes 2097168 | tf_op jit(solution)/shard_map/all_gather | solution.py:76
  307.9 6.3 %fusion.7 = f32[256,128]{0,1:T(8,128)S(1)} fusion(f32[256,128]{0,1:T(8,128)S(1)} %copy.22, f32[4096,128]{1,0:T(8,128)} %all-gather.6.cloned.1.call-done, f32[256,4096]{0,1:T(8,128)} %bitcast.37), kind=kOutput, calls=%fused_computation.6 | convolution fusion | flops 1610645504 | bytes 6553600 | tf_op jit(solution)/shard_map/dot_general | solution.py:38
  314.2 0.8 copy.26
  (15 shorter events, 1.3 us)
Async XLA Ops:
  7.2 111.6 %all-gather.4.cloned.1.call-start = ((), (), s32[]{:S(2)}) async-start(), calls=%async_computation.7 | async-start | bytes 4456448 | tf_op jit(solution)/shard_map/all_gather | solution.py:30
  8.9 244.6 %all-gather.8.cloned.1.call-start = ((), (), s32[]{:S(2)}) async-start(), calls=%async_computation.9 | async-start | bytes 2228224 | tf_op jit(solution)/shard_map/all_gather | solution.py:78
  125.7 46.7 %copy-start = (f32[256,128]{0,1:T(8,128)S(1)}, f32[256,128]{0,1:T(8,128)}, u32[]{:S(2)}) copy-start(f32[256,128]{0,1:T(8,128)} %fusion.4) | copy-start | bytes 393220
  132.1 55.3 %copy-start.1 = (f32[256,128]{1,0:T(8,128)S(1)}, f32[256,128]{1,0:T(8,128)}, u32[]{:S(2)}) copy-start(f32[256,128]{1,0:T(8,128)} %param.5) | copy-start | bytes 393220
  168.4 13.0 %all-to-all-start.4 = ((f32[32,8,128]{2,1,0:T(8,128)}), f32[32,8,128]{2,1,0:T(8,128)S(1)}, u32[]{:S(2)}, u32[]{:S(2)}) async-start(f32[32,8,128]{2,1,0:T(8,128)} %all_to_all.38), calls=%async_computation.4 | async-start | bytes 262144 | tf_op jit(solution)/shard_map/all_to_all | solution.py:74
  182.9 51.9 %all-to-all-start.5 = ((f32[16,256,128]{2,1,0:T(8,128)}), f32[16,256,128]{2,1,0:T(8,128)S(1)}, u32[]{:S(2)}, u32[]{:S(2)}) async-start(f32[16,256,128]{2,1,0:T(8,128)} %broadcast_in_dim.14), calls=%async_computation.5 | async-start | bytes 4194304 | tf_op jit(solution)/shard_map/all_to_all | solution.py:12
  186.6 121.2 %all-gather.6.cloned.1.call-start = ((), (), s32[]{:S(2)}) async-start(), calls=%async_computation.8 | async-start | bytes 2228224 | tf_op jit(solution)/shard_map/all_gather | solution.py:76
Sparse Core Ops, SparseCore 0:
  11.1 107.5 all-gather.3
  125.9 90.7 all-gather.7
  220.4 87.4 all-gather.5
where the time goes:
time: 325 us; the launch traced here: 322 us
  waiting for transfers between devices  130 us (40%)
  blocking collectives  117 us (36%)
  matrix products  29.9 us (9%)
  local copies, waits for them, and re-layouts  21.3 us (7%)
  between operations  13.8 us (4%)
  starting transfers between devices  7.91 us (2%)
    all_to_all x3, blocking collectives, from_everyone(): return lax.all_to_all(copies, axis, split_axis=0, concat_axis=0, tiled=True)  80.5 us
    all_to_all x1, waiting for transfers between devices, from_everyone(): return lax.all_to_all(copies, axis, split_axis=0, concat_axis=0, tiled=True)  47.3 us
    all_gather x1, waiting for transfers between devices, on_device(): lax.all_gather(turned, 'row', axis=0, tiled=True)  44.2 us
    dot_general x4, matrix products, matmul(): jnp.dot(left, right, preferred_element_type=jnp.float32, precision=lax.Pr...  29.9 us
    all_gather x1, waiting for transfers between devices, side_by_side(): whole, at, done = (lax.all_gather(both, axis, axis=dim, tiled=True), 0, [])  29.7 us
    all_to_all x1, blocking collectives, on_device(): lax.all_to_all(lax.all_to_all(split_pieces(product, groups), 'row', split...  22.9 us
    all_to_all x1, blocking collectives, on_device(): lax.all_to_all(split_pieces(product, groups), 'row', split_axis=0, concat...  13.3 us
    transpose x2, local copies, waits for them, and re-layouts, in_order(): parts = jnp.moveaxis(parts, 0, dim)  11.3 us
  transfers between devices with their start and end apart: 5, of which 4 were waited for; matrix products, arithmetic and copies ran while one was open for 12% of the time, Pallas kernels for 0%

commit v1 on v0

v1 whole, which is shorter than its diff:
```python
import functools
import itertools

import jax
import jax.numpy as jnp
from jax import lax
from jax.experimental import pallas as pl
from jax.experimental.pallas import tpu as pltpu
from jax.sharding import PartitionSpec as P

MESH = pl.DeviceIdType.MESH
B, H = 256, 128
RINGS = ((0, 0), (0, 1), (1, 0), (1, 1))
BF, F32 = jnp.bfloat16, jnp.float32
COPIES = 130


def length(g, d):
    return 4 if g == d else 3


def sign(d):
    return 1 if d == 0 else -1


def wrap(v):
    return lax.rem(v + 16, 8)


def halves(v):
    hi = v.astype(BF)
    return hi, (v - hi.astype(F32)).astype(BF)


def dot(a, b):
    return jnp.dot(a, b, preferred_element_type=F32)


def dot_t(a, b):
    return lax.dot_general(a, b, (((1,), (1,)), ((), ())), preferred_element_type=F32)


def kernel(a_ref, x_ref, q_ref, n_ref, f_ref, ar, ac, xc, sr, sc, part, swap, run, last, s_own, t_own, acc2, acc1, p2, send, recv):
    row, col = lax.axis_index("row"), lax.axis_index("col")
    xh, y = row // 8, lax.rem(row, 8)
    z, xl, core = col // 4, lax.rem(col // 2, 2), lax.rem(col, 2)
    ids = itertools.count()
    sent = []

    y_dev = [(xh * 8 + wrap(y + sign(d)), col) for d in (0, 1)]
    z_dev = [(row, wrap(z + sign(d)) * 4 + xl * 2 + core) for d in (0, 1)]
    hi_dev = ((1 - xh) * 8 + y, col)
    lo_dev = (row, z * 4 + (1 - xl) * 2 + core)
    mate = (row, z * 4 + xl * 2 + (1 - core))

    barrier = pltpu.get_barrier_semaphore()
    greeted = (*y_dev, *z_dev, hi_dev, lo_dev, mate)
    for device in greeted:
        pl.semaphore_signal(barrier, inc=1, device_id=device, device_id_type=MESH)
    pl.semaphore_wait(barrier, len(greeted))

    def copy(k, src, dst, device):
        return pltpu.make_async_remote_copy(
            src_ref=src, dst_ref=dst, send_sem=send.at[k], recv_sem=recv.at[k], device_id=device, device_id_type=MESH
        )

    def start(k, src, dst, device):
        c = copy(k, src, dst, device)
        c.start()
        sent.append(c)

    def arrived(k, dst):
        copy(k, dst, dst, mate).wait_recv()

    class Panel:
        def __init__(self, buf, own, at, pos, devices, partner, mated):
            self.buf, self.own, self.at, self.pos = buf, own, at, pos
            self.devices, self.partner, self.mated = devices, partner, mated
            self.kx = next(ids)
            self.k = {(g, d, s): next(ids) for g, d in RINGS for s in range(1, length(g, d) + 1)}
            self.km = {e: next(ids) for e in ("own", "x", *self.k)} if mated else {}

        def slot(self, g, p, other=False):
            return self.buf.at[self.at(g, p, other)]

        def place(self, g, d, s):
            return g, wrap(self.pos - sign(d) * s)

        def where(self, e):
            if e == "own":
                return 0, self.pos
            return (1, self.pos) if e == "x" else self.place(*e)

        def to_mate(self, e):
            if self.mated:
                here = self.slot(*self.where(e))
                start(self.km[e], self.own if e == "own" else here, here, mate)

        def from_mate(self):
            for e, k in self.km.items():
                arrived(k, self.slot(*self.where(e), True))

        def exchange(self):
            start(self.kx, self.own, self.slot(0, self.pos), self.partner)

        def launch(self):
            for d in (0, 1):
                self.forward(0, d, 1)
            self.to_mate("own")

        def relaunch(self):
            arrived(self.kx, self.slot(1, self.pos))
            for d in (0, 1):
                self.forward(1, d, 1)
            self.to_mate("x")

        def forward(self, g, d, s):
            there = self.slot(*self.place(g, d, s - 1))
            start(self.k[g, d, s], self.own if g == 0 and s == 1 else there, there, self.devices[d])

        def step(self, s):
            for g, d in RINGS:
                if s <= length(g, d):
                    arrived(self.k[g, d, s], self.slot(*self.place(g, d, s)))
                    if s < length(g, d):
                        self.forward(g, d, s + 1)
                    self.to_mate((g, d, s))

    def row_at(g, p, other):
        lo = xl if g == 0 else 1 - xl
        c = 1 - core if other else core
        return p * 4 + lo * 2 + c

    def col_at(g, p, other):
        return (xh if g == 0 else 1 - xh) * 8 + p

    def row_panel(buf, own):
        return Panel(buf, own, row_at, z, z_dev, lo_dev, True)

    def col_panel(buf, own):
        return Panel(buf, own, col_at, y, y_dev, hi_dev, False)

    def multiply(left, right, out):
        acc2[...] = jnp.zeros_like(acc2)
        acc1[...] = jnp.zeros_like(acc1)

        def body(i, carry):
            lh, ll = halves(jnp.concatenate([left[4 * i + j] for j in range(4)], axis=1))
            rh, rl = halves(jnp.concatenate([right[2 * i + j] for j in range(2)], axis=0))
            acc2[...] += dot(lh, jnp.concatenate([rh, rl], axis=1))
            acc1[...] += dot(ll, rh)
            return carry

        lax.fori_loop(0, 8, body, 0)
        out[...] = acc2[:, :H] + acc2[:, H:] + acc1[...]

    a_row, a_col, x_col = row_panel(ar, a_ref), col_panel(ac, a_ref), col_panel(xc, x_ref)
    s_row, s_col = row_panel(sr, s_own), col_panel(sc, s_own)

    a_col.launch()
    a_row.launch()
    a_col.exchange()
    a_row.exchange()
    x_col.exchange()
    ac[row] = a_ref[...]
    ar[col] = a_ref[...]
    xc[row] = x_ref[...]
    a_col.relaunch()
    a_row.relaunch()
    for s in range(1, 5):
        a_col.step(s)
        a_row.step(s)
        if s == 3:
            x_col.launch()
    x_col.relaunch()
    a_row.from_mate()
    multiply(ar, ac, s_own)
    s_row.exchange()
    s_row.launch()
    s_col.exchange()
    sr[col] = s_own[...]
    sc[row] = s_own[...]
    x_col.step(1)
    s_row.relaunch()
    for s in range(1, 5):
        if s > 1:
            x_col.step(s)
        s_row.step(s)
        if s == 3:
            s_col.launch()
    s_col.relaunch()
    multiply(ar, xc, t_own)

    hi, lo = halves(t_own[...])
    p2[...] = jnp.concatenate([hi, lo], axis=1)
    order = (4, 3, 5, 2, 6, 1, 7, 0)
    kn = {o: next(ids) for o in order}

    def part_of(o):
        zz = wrap(z + o)
        for l in (0, 1):
            bh, bl = halves(ac[2 * zz + l])
            both = dot_t(p2[...], jnp.concatenate([bh, bh], axis=1)) + dot_t(p2[:, :H], bl)
            part[0, zz, l] = both[:, :H]
            part[1, zz, l] = both[:, H:]
        start(kn[o], part.at[1 - core, zz], swap.at[zz], mate)

    for o in order:
        part_of(o)

    kr = {(g, d, s): next(ids) for g, d in RINGS for s in range(1, length(g, d) + 1)}
    at_run = {e: i for i, e in enumerate(kr)}
    have = set()

    def share(g, off):
        zz = wrap(z + off)
        if off % 8 not in have:
            have.add(off % 8)
            arrived(kn[off % 8], swap.at[zz])
        l = xl if g == 0 else 1 - xl
        return part[core, zz, l] + swap[zz, l]

    for g, d in reversed(RINGS):
        off = sign(d) * length(g, d)
        l = xl if g == 0 else 1 - xl
        zz = wrap(z + off)
        part[core, zz, l] = share(g, off)
        start(kr[g, d, 1], part.at[core, zz, l], run.at[at_run[g, d, 1]], z_dev[d])

    for s in range(1, 5):
        s_col.step(s)
        for g, d in reversed(RINGS):
            if s < length(g, d):
                here = run.at[at_run[g, d, s]]
                arrived(kr[g, d, s], here)
                here[...] += share(g, sign(d) * (length(g, d) - s))
                start(kr[g, d, s + 1], here, run.at[at_run[g, d, s + 1]], z_dev[d])

    def total(g):
        both = [run.at[at_run[g, d, length(g, d)]] for d in (0, 1)]
        for d in (0, 1):
            arrived(kr[g, d, length(g, d)], both[d])
        return both[0][...] + both[1][...] + share(g, 0)

    k_last = next(ids)
    t_own[...] = total(1)
    start(k_last, t_own, last, lo_dev)
    n_ref[...] = total(0) + q_ref[...]
    s_row.from_mate()
    multiply(sr, sc, f_ref)
    arrived(k_last, last)
    n_ref[...] += last[...]
    for c in sent:
        c.wait_send()
    assert next(ids) == COPIES


def on_device(operator, state, source):
    block = jax.ShapeDtypeStruct((B, H), F32)
    vmem = pl.BlockSpec(memory_space=pltpu.VMEM)

    def blocks(*lead):
        return pltpu.VMEM((*lead, B, H), F32)

    return pl.pallas_call(
        kernel,
        out_shape=(block, block),
        in_specs=[vmem] * 3,
        out_specs=(vmem, vmem),
        scratch_shapes=[
            blocks(32),
            blocks(16),
            blocks(16),
            blocks(32),
            blocks(16),
            blocks(2, 8, 2),
            blocks(8, 2),
            blocks(14),
            blocks(),
            blocks(),
            blocks(),
            pltpu.VMEM((B, B), F32),
            blocks(),
            pltpu.VMEM((B, B), BF),
            pltpu.SemaphoreType.DMA((COPIES,)),
            pltpu.SemaphoreType.DMA((COPIES,)),
        ],
        compiler_params=pltpu.CompilerParams(collective_id=0, has_side_effects=True, vmem_limit_bytes=56 << 20),
        name="smith",
    )(operator, state, source)


def solution(mesh):
    spec = P("row", "col")
    return jax.shard_map(on_device, mesh=mesh, in_specs=(spec, spec, spec), out_specs=(spec, spec), check_vma=False)
```

time: 325 us -> 109 us (0.34); the launches traced: 322 us -> 109 us
  waiting for transfers between devices: 130 us -> 0 us
  blocking collectives: 117 us -> 0 us
  Pallas kernels: 0 us -> 106 us
  matrix products: 29.9 us -> 0 us
  local copies, waits for them, and re-layouts: 21.3 us -> 2.26 us
  between operations: 13.8 us -> 0.65 us
  starting transfers between devices: 7.91 us -> 0 us
    all_to_all x5 -> x0, blocking collectives: 117 us -> none  [the longest x3 80.5 us: from_everyone(): return lax.all_to_all(copies, axis, split_axis=0, concat_axis=0, tiled=True)]
    pallas_call x0 -> x1, Pallas kernels: none -> 106 us  [on_device(): pl.pallas_call(kernel, out_shape=(block, block), in_specs=[vmem] * 3, out...]
    all_gather x3 -> x0, waiting for transfers between devices: 73.9 us -> none  [the longest x1 44.2 us: on_device(): lax.all_gather(turned, 'row', axis=0, tiled=True)]
    all_to_all x2 -> x0, waiting for transfers between devices: 56.2 us -> none  [the longest x1 47.3 us: from_everyone(): return lax.all_to_all(copies, axis, split_axis=0, concat_axis=0, tiled=True)]
    dot_general x4 -> x0, matrix products: 29.9 us -> none  [matmul(): jnp.dot(left, right, preferred_element_type=jnp.float32, precision=lax.Pr...]
    transpose x3 -> x0, local copies, waits for them, and re-layouts: 11.9 us -> none  [the longest x2 11.3 us: in_order(): parts = jnp.moveaxis(parts, 0, dim)]
    all_to_all x2 -> x0, starting transfers between devices: 7.79 us -> none  [the longest x1 4.07 us: on_device(): lax.all_to_all(moved, 'row', split_axis=0, concat_axis=0, tiled=True)]
    all_to_all x2 -> x0, local copies, waits for them, and re-layouts: 4.81 us -> none  [from_everyone(): return lax.all_to_all(copies, axis, split_axis=0, concat_axis=0, tiled=True)]
  transfers between devices with their start and end apart: 5 -> 0, of which waited for: 4 -> 0; matrix products, arithmetic and copies ran while one was open for 12% -> 0% of each run, Pallas kernels for 0% -> 0%
where the time goes in v1:
time: 109 us
  Pallas kernels  106 us (97%)
  local copies, waits for them, and re-layouts  2.26 us (2%)
    pallas_call x1, Pallas kernels, on_device(): pl.pallas_call(kernel, out_shape=(block, block), in_specs=[vmem] * 3, out...  106 us
    unnamed x4, local copies, waits for them, and re-layouts  2.26 us

profile of v1, /device:TPU:1, one launch (start us, length us, event | category | flops | bytes accessed | tf_op | source)
XLA Modules:
  0.0 109.2 jit_solution(10875537594745516154)
XLA Ops:
  0.6 106.3 %smith.1 = (f32[256,128]{1,0:T(8,128)}, f32[256,128]{1,0:T(8,128)}) custom-call(f32[256,128]{1,0:T(8,128)} %a_ref.1, f32[256,128]{1,0:T(8,128)} %x_ref.1, f32[256,128]{1,0:T(8,128)} %q_ref.1), custom_call_target="tpu_custom_call" | custom-call | tf_op jit(solution)/shard_map/smith/pallas_call | solution.py:265
  107.0 0.0 copy-start
  107.0 1.6 %copy.7 = f32[256,128]{1,0:T(8,128)} copy(f32[256,128]{1,0:T(8,128)} %get-tuple-element.4) | data formatting | bytes 262144
  108.6 0.0 copy-done
  108.6 0.7 copy.8
Async XLA Ops:
  107.0 1.6 %copy-start = (f32[256,128]{1,0:T(8,128)S(1)}, f32[256,128]{1,0:T(8,128)}, u32[]{:S(2)}) copy-start(f32[256,128]{1,0:T(8,128)} %get-tuple-element.5) | copy-start | bytes 393220

commit v2 on v1

v2 whole, which is shorter than its diff:
```python
import functools
import itertools

import jax
import jax.numpy as jnp
from jax import lax
from jax.experimental import pallas as pl
from jax.experimental.pallas import tpu as pltpu
from jax.sharding import PartitionSpec as P

MESH = pl.DeviceIdType.MESH
B, H = 256, 128
RINGS = ((0, 0), (0, 1), (1, 0), (1, 1))
BF, F32 = jnp.bfloat16, jnp.float32
PARTS = 2
SHORT = {"a_row": (4, 4), "a_col": (4, 4), "x_col": (4, 4), "s_row": (2, 2), "s_col": (4, 4), "sum": (4, 4)}


def reach(d, p):
    return 4 if d == p else 3


def hops(short, g, d, p):
    return min(short[d == p], reach(d, p)) if g else reach(d, p)


def events(short):
    return [(g, d, s, p) for g, d in RINGS for p in range(PARTS) for s in range(1, hops(short, g, d, p) + 1)]


def far(short):
    return [(d, s, p) for s in range(1, 5) for d in (0, 1) for p in range(PARTS) if hops(short, 1, d, p) < s <= reach(d, p)]


def sign(d):
    return 1 if d == 0 else -1


def wrap(v):
    return lax.rem(v + 16, 8)


def copies():
    count = {name: len(events(short)) + len(far(short)) for name, short in SHORT.items()}
    return sum(count.values()) + 5 * PARTS + 2 + 8 + 1


def piece(ref, p):
    return ref.at[pl.ds(p * (B // PARTS), B // PARTS)]


def halves(v):
    hi = v.astype(BF)
    return hi, (v - hi.astype(F32)).astype(BF)


def dot(a, b):
    return jnp.dot(a, b, preferred_element_type=F32)


def dot_t(a, b):
    return lax.dot_general(a, b, (((1,), (1,)), ((), ())), preferred_element_type=F32)


def kernel(a_ref, x_ref, q_ref, n_ref, f_ref, ar, ac, xc, sr, sc, part, swap, run, loan, last, s_own, t_own, acc2, acc1, p2, send, recv):
    row, col = lax.axis_index("row"), lax.axis_index("col")
    xh, y = row // 8, lax.rem(row, 8)
    z, xl, core = col // 4, lax.rem(col // 2, 2), lax.rem(col, 2)
    ids, groups = itertools.count(), itertools.count()

    y_dev = [(xh * 8 + wrap(y + sign(d)), col) for d in (0, 1)]
    z_dev = [(row, wrap(z + sign(d)) * 4 + xl * 2 + core) for d in (0, 1)]
    hi_dev = ((1 - xh) * 8 + y, col)
    lo_dev = (row, z * 4 + (1 - xl) * 2 + core)
    mate = (row, z * 4 + xl * 2 + (1 - core))

    barrier = pltpu.get_barrier_semaphore()
    across = [(row, wrap(z + sign(d)) * 4 + (1 - xl) * 2 + core) for d in (0, 1)]
    greeted = (*y_dev, *z_dev, *across, hi_dev, lo_dev, mate)
    for device in greeted:
        pl.semaphore_signal(barrier, inc=1, device_id=device, device_id_type=MESH)
    pl.semaphore_wait(barrier, len(greeted))

    def copy(k, src, dst, device, group=0):
        return pltpu.make_async_remote_copy(
            src_ref=src, dst_ref=dst, send_sem=send.at[group], recv_sem=recv.at[k], device_id=device, device_id_type=MESH
        )

    def start(group, k, src, dst, device):
        copy(k, src, dst, device, group).start()

    def arrived(k, dst):
        copy(k, dst, dst, mate).wait_recv()

    def all_sent(group, as_much):
        copy(0, as_much, as_much, mate, group).wait_send()

    class Panel:
        def __init__(self, buf, own, at, pos, devices, partner, mated, short):
            self.buf, self.own, self.at, self.pos = buf, own, at, pos
            self.devices, self.partner, self.mated, self.short = devices, partner, mated, short
            self.kx = [next(ids) for _ in range(PARTS)]
            self.group = next(groups)
            self.k = {e: next(ids) for e in events(short)}
            self.kf = {e: next(ids) for e in far(short)}
            self.km = next(ids) if mated else None

        def slot(self, g, d, s, p):
            return piece(self.buf.at[self.at(g, wrap(self.pos - sign(d) * s))], p)

        def to_mate(self, e, src=None):
            if self.mated:
                here = self.slot(*e)
                start(self.group, self.km, here if src is None else src, here, mate)

        def from_mate(self):
            arrived(self.km, self.buf.at[pl.ds(0, 16)])

        def all_sent(self):
            all_sent(self.group, self.buf.at[pl.ds(0, 31 if self.mated else 15)])

        def exchange(self):
            for p in range(PARTS):
                start(self.group, self.kx[p], piece(self.own, p), self.slot(0, 0, 0, p), self.partner)

        def forward(self, g, d, s, p):
            there = self.slot(g, d, s - 1, p)
            start(self.group, self.k[g, d, s, p], piece(self.own, p) if g == 0 and s == 1 else there, there, self.devices[d])

        def launch(self):
            for p in range(PARTS):
                for d in (0, 1):
                    self.forward(0, d, 1, p)
            for p in range(PARTS):
                self.to_mate((0, 0, 0, p), piece(self.own, p))

        def relaunch(self, p):
            arrived(self.kx[p], self.slot(1, 0, 0, p))
            for d in (0, 1):
                if hops(self.short, 1, d, p):
                    self.forward(1, d, 1, p)
            self.to_mate((1, 0, 0, p))

        def hop(self, g, d, s, p):
            e = (g, d, s, p)
            if e not in self.k:
                return
            here = self.slot(*e)
            arrived(self.k[e], here)
            if (g, d, s + 1, p) in self.k:
                self.forward(g, d, s + 1, p)
            if g == 0 and e[1:] in self.kf:
                start(self.group, self.kf[e[1:]], here, here, self.partner)
            self.to_mate(e)

        def step(self, s, g, p):
            if s == 1 and g == 0:
                self.relaunch(p)
            for d in (0, 1):
                self.hop(g, d, s, p)

        def finish(self, steps=(1, 2, 3, 4)):
            for e, k in self.kf.items():
                if e[1] in steps:
                    arrived(k, self.slot(1, *e))
                    self.to_mate((1, *e))

    def step(s, *panels):
        for g in (0, 1):
            for p in range(PARTS):
                for panel in panels:
                    panel.step(s, g, p)

    def row_at(g, p):
        lo = xl if g == 0 else 1 - xl
        return p * 4 + lo * 2 + core

    def col_at(g, p):
        return (xh if g == 0 else 1 - xh) * 8 + p

    def row_panel(buf, own, short):
        return Panel(buf, own, row_at, z, z_dev, lo_dev, True, short)

    def col_panel(buf, own, short):
        return Panel(buf, own, col_at, y, y_dev, hi_dev, False, short)

    def clear():
        acc2[...] = jnp.zeros_like(acc2)
        acc1[...] = jnp.zeros_like(acc1)

    def terms(left, right, first, count):
        def body(i, carry):
            here = wrap(y + i + first)
            lh, ll = halves(jnp.concatenate([left[2 * here + j] for j in (0, 1, 16, 17)], axis=1))
            rh, rl = halves(jnp.concatenate([right[here + j] for j in (0, 8)], axis=0))
            acc2[...] += dot(lh, jnp.concatenate([rh, rl], axis=1))
            acc1[...] += dot(ll, rh)
            return carry

        lax.fori_loop(0, count, body, 0)

    def value():
        return acc2[:, :H] + acc2[:, H:] + acc1[...]

    a_row, a_col = row_panel(ar, a_ref, SHORT["a_row"]), col_panel(ac, a_ref, SHORT["a_col"])
    s_row, s_col = row_panel(sr, s_own, SHORT["s_row"]), col_panel(sc, s_own, SHORT["s_col"])
    x_col = col_panel(xc, x_ref, SHORT["x_col"])

    a_col.launch()
    a_row.launch()
    a_col.exchange()
    a_row.exchange()
    ac[row] = a_ref[...]
    ar[col] = a_ref[...]
    xc[row] = x_ref[...]
    for s in range(1, 5):
        step(s, a_col, a_row)
        if s == 2:
            x_col.exchange()
        if s == 3:
            x_col.launch()
    a_row.finish()
    a_col.finish()
    a_row.from_mate()
    clear()
    terms(ar, ac, 0, 8)
    s_own[...] = value()
    s_row.launch()
    s_row.exchange()
    s_col.exchange()
    sr[col] = s_own[...]
    sc[row] = s_own[...]
    for s in range(1, 5):
        step(s, x_col, s_row)
        if s == 3:
            s_col.launch()
            clear()
            terms(ar, xc, -3, 7)
    x_col.finish()
    terms(ar, xc, 4, 1)
    t_own[...] = value()

    hi, lo = halves(t_own[...])
    p2[...] = jnp.concatenate([hi, lo], axis=1)
    order = (4, 3, 5, 2, 6, 1, 7, 0)
    kn = {o: next(ids) for o in order}
    g_part, g_sum = next(groups), next(groups)

    def part_of(o):
        zz = wrap(z + o)
        for l in (0, 1):
            bh, bl = halves(ac[2 * zz + l])
            both = dot_t(p2[...], jnp.concatenate([bh, bh], axis=1)) + dot_t(p2[:, :H], bl)
            part[0, zz, l] = both[:, :H]
            part[1, zz, l] = both[:, H:]
        start(g_part, kn[o], part.at[1 - core, zz], swap.at[zz], mate)

    short = SHORT["sum"]
    runs, lent = events(short), far(short)
    kr = {e: next(ids) for e in runs}
    kl = {e: next(ids) for e in lent}
    have = set()

    def share(g, d, s, p):
        zz = wrap(z + sign(d) * s)
        o = sign(d) * s % 8
        if o not in have:
            have.add(o)
            arrived(kn[o], swap.at[zz])
        l = xl if g == 0 else 1 - xl
        return piece(part.at[core, zz, l], p), piece(swap.at[zz, l], p)

    def lend(d, s, p):
        mine, theirs = share(1, d, s, p)
        mine[...] += theirs[...]
        start(g_sum, kl[d, s, p], mine, loan.at[lent.index((d, s, p))], lo_dev)

    def added(value, g, d, s, p):
        mine, theirs = share(g, d, s, p)
        value = mine[...] + theirs[...] if value is None else value + (mine[...] + theirs[...])
        if g == 0 and (d, s, p) in kl:
            here = loan.at[lent.index((d, s, p))]
            arrived(kl[d, s, p], here)
            value = value + here[...]
        return value

    def relay(g, d, p, s):
        n = hops(short, g, d, p)
        if not 1 <= s <= n:
            return
        if s == n:
            here = share(g, d, s, p)[0]
            here[...] = added(None, g, d, s, p)
        else:
            e = (g, d, n - s, p)
            here = run.at[runs.index(e)]
            arrived(kr[e], here)
            here[...] = added(here[...], g, d, s, p)
        e = (g, d, n - s + 1, p)
        there = across[d] if g == 1 and s == 1 else z_dev[d]
        start(g_sum, kr[e], here, run.at[runs.index(e)], there)

    for o in order[:3]:
        part_of(o)
    for d, s, p in reversed(lent):
        lend(d, s, p)
    for o in order[3:]:
        part_of(o)

    def relays(g, back):
        for p in range(PARTS):
            for d in (0, 1):
                relay(g, d, p, hops(short, g, d, p) - back)

    k_last = next(ids)
    relays(1, 0)
    relays(0, 0)
    for p in range(PARTS):
        mine, theirs = share(1, 0, 0, p)
        mine[...] += theirs[...]
    start(g_sum, k_last, part.at[core, z, 1 - xl], last, lo_dev)
    for back in range(1, 4):
        for g in (1, 0):
            for p in range(PARTS):
                s_col.step(back, 1 - g, p)
                for d in (0, 1):
                    relay(g, d, p, hops(short, g, d, p) - back)
        if back == 2:
            s_row.finish()
            s_row.from_mate()
    clear()
    terms(sr, sc, -3, 7)
    step(4, s_col)
    s_col.finish()
    terms(sr, sc, 4, 1)
    f_ref[...] = value()
    arrived(k_last, last)
    n_ref[...] = q_ref[...] + last[...]
    for p in range(PARTS):
        here = piece(n_ref, p)
        here[...] = added(here[...], 0, 0, 0, p)
        for g in (1, 0):
            for d in (0, 1):
                e = (g, d, hops(short, g, d, p), p)
                arrived(kr[e], run.at[runs.index(e)])
                here[...] += run[runs.index(e)]
    for panel in (a_row, a_col, x_col, s_row, s_col):
        panel.all_sent()
    all_sent(g_part, swap.at[...])
    all_sent(g_sum, ar.at[pl.ds(0, 15)])
    assert next(ids) == copies()


def on_device(operator, state, source):
    block = jax.ShapeDtypeStruct((B, H), F32)
    vmem = pl.BlockSpec(memory_space=pltpu.VMEM)

    def blocks(*lead):
        return pltpu.VMEM((*lead, B, H), F32)

    return pl.pallas_call(
        kernel,
        out_shape=(block, block),
        in_specs=[vmem] * 3,
        out_specs=(vmem, vmem),
        scratch_shapes=[
            blocks(32),
            blocks(16),
            blocks(16),
            blocks(32),
            blocks(16),
            blocks(2, 8, 2),
            blocks(8, 2),
            pltpu.VMEM((len(events(SHORT["sum"])), B // PARTS, H), F32),
            pltpu.VMEM((max(1, len(far(SHORT["sum"]))), B // PARTS, H), F32),
            blocks(),
            blocks(),
            blocks(),
            pltpu.VMEM((B, B), F32),
            blocks(),
            pltpu.VMEM((B, B), BF),
            pltpu.SemaphoreType.DMA((7,)),
            pltpu.SemaphoreType.DMA((copies(),)),
        ],
        compiler_params=pltpu.CompilerParams(collective_id=0, has_side_effects=True, vmem_limit_bytes=56 << 20),
        name="smith",
    )(operator, state, source)


def solution(mesh):
    spec = P("row", "col")
    return jax.shard_map(on_device, mesh=mesh, in_specs=(spec, spec, spec), out_specs=(spec, spec), check_vma=False)
```

time: 109 us -> 96.7 us (0.89)
  Pallas kernels: 106 us -> 93.6 us
    pallas_call x1, Pallas kernels: 106 us -> 93.6 us  [on_device(): pl.pallas_call(kernel, out_shape=(block, block), in_specs=[vmem] * 3, out...]
where the time goes in v2:
time: 96.7 us; the launch traced here: 96.5 us
  Pallas kernels  93.6 us (97%)
  local copies, waits for them, and re-layouts  2.26 us (2%)
    pallas_call x1, Pallas kernels, on_device(): pl.pallas_call(kernel, out_shape=(block, block), in_specs=[vmem] * 3, out...  93.6 us
    unnamed x4, local copies, waits for them, and re-layouts  2.26 us

profile of v2, /device:TPU:1, one launch (start us, length us, event | category | flops | bytes accessed | tf_op | source)
XLA Modules:
  0.0 96.5 jit_solution(6115325678703200973)
XLA Ops:
  0.6 93.6 %smith.1 = (f32[256,128]{1,0:T(8,128)}, f32[256,128]{1,0:T(8,128)}) custom-call(f32[256,128]{1,0:T(8,128)} %a_ref.1, f32[256,128]{1,0:T(8,128)} %x_ref.1, f32[256,128]{1,0:T(8,128)} %q_ref.1), custom_call_target="tpu_custom_call" | custom-call | tf_op jit(solution)/shard_map/smith/pallas_call | solution.py:361
  94.2 0.0 copy-start
  94.2 1.6 %copy.7 = f32[256,128]{1,0:T(8,128)} copy(f32[256,128]{1,0:T(8,128)} %get-tuple-element.4) | data formatting | bytes 262144
  95.9 0.0 copy-done
  95.9 0.7 copy.8
Async XLA Ops:
  94.2 1.6 %copy-start = (f32[256,128]{1,0:T(8,128)S(1)}, f32[256,128]{1,0:T(8,128)}, u32[]{:S(2)}) copy-start(f32[256,128]{1,0:T(8,128)} %get-tuple-element.5) | copy-start | bytes 393220

commit v3 on v2

--- a/solution.py
+++ b/solution.py
@@ -13,6 +13,36 @@
 RINGS = ((0, 0), (0, 1), (1, 0), (1, 1))
 BF, F32 = jnp.bfloat16, jnp.float32
 PARTS = 2
+ORDER = (
+    "begin",
+    "a1",
+    "xe",
+    "a2",
+    "xl",
+    "a3",
+    "a4",
+    "x1",
+    "square",
+    "x2r1",
+    "x3",
+    "cl",
+    "xn",
+    "r2",
+    "x4",
+    "product",
+    "parts",
+    "sums",
+    "r3",
+    "c1b1",
+    "r4",
+    "c2b2",
+    "rows",
+    "c3b3",
+    "cn",
+    "c4",
+    "fourth",
+    "next",
+)
 SHORT = {"a_row": (4, 4), "a_col": (4, 4), "x_col": (4, 4), "s_row": (2, 2), "s_col": (4, 4), "sum": (4, 4)}
 
 
@@ -206,42 +236,38 @@
     s_row, s_col = row_panel(sr, s_own, SHORT["s_row"]), col_panel(sc, s_own, SHORT["s_col"])
     x_col = col_panel(xc, x_ref, SHORT["x_col"])
 
-    a_col.launch()
-    a_row.launch()
-    a_col.exchange()
-    a_row.exchange()
-    ac[row] = a_ref[...]
-    ar[col] = a_ref[...]
-    xc[row] = x_ref[...]
-    for s in range(1, 5):
-        step(s, a_col, a_row)
-        if s == 2:
-            x_col.exchange()
-        if s == 3:
-            x_col.launch()
-    a_row.finish()
-    a_col.finish()
-    a_row.from_mate()
-    clear()
-    terms(ar, ac, 0, 8)
-    s_own[...] = value()
-    s_row.launch()
-    s_row.exchange()
-    s_col.exchange()
-    sr[col] = s_own[...]
-    sc[row] = s_own[...]
-    for s in range(1, 5):
-        step(s, x_col, s_row)
-        if s == 3:
-            s_col.launch()
-            clear()
-            terms(ar, xc, -3, 7)
-    x_col.finish()
-    terms(ar, xc, 4, 1)
-    t_own[...] = value()
-
-    hi, lo = halves(t_own[...])
-    p2[...] = jnp.concatenate([hi, lo], axis=1)
+    def begin():
+        a_col.launch()
+        a_row.launch()
+        a_col.exchange()
+        a_row.exchange()
+        ac[row] = a_ref[...]
+        ar[col] = a_ref[...]
+        xc[row] = x_ref[...]
+
+    def square():
+        a_row.finish()
+        a_col.finish()
+        a_row.from_mate()
+        clear()
+        terms(ar, ac, 0, 8)
+        s_own[...] = value()
+        s_row.launch()
+        s_row.exchange()
+        s_col.exchange()
+        sr[col] = s_own[...]
+        sc[row] = s_own[...]
+
+    def near(left, right):
+        clear()
+        terms(left, right, -3, 7)
+
+    def product():
+        x_col.finish()
+        terms(ar, xc, 4, 1)
+        hi, lo = halves(value())
+        p2[...] = jnp.concatenate([hi, lo], axis=1)
+
     order = (4, 3, 5, 2, 6, 1, 7, 0)
     kn = {o: next(ids) for o in order}
     g_part, g_sum = next(groups), next(groups)
@@ -300,59 +326,85 @@
         there = across[d] if g == 1 and s == 1 else z_dev[d]
         start(g_sum, kr[e], here, run.at[runs.index(e)], there)
 
-    for o in order[:3]:
-        part_of(o)
-    for d, s, p in reversed(lent):
-        lend(d, s, p)
-    for o in order[3:]:
-        part_of(o)
-
-    def relays(g, back):
+    def parts():
+        for o in order[:3]:
+            part_of(o)
+        for d, s, p in reversed(lent):
+            lend(d, s, p)
+        for o in order[3:]:
+            part_of(o)
+
+    k_last = next(ids)
+
+    def sums():
+        advance([("b", 0)])
         for p in range(PARTS):
-            for d in (0, 1):
-                relay(g, d, p, hops(short, g, d, p) - back)
-
-    k_last = next(ids)
-    relays(1, 0)
-    relays(0, 0)
-    for p in range(PARTS):
-        mine, theirs = share(1, 0, 0, p)
-        mine[...] += theirs[...]
-    start(g_sum, k_last, part.at[core, z, 1 - xl], last, lo_dev)
-    for back in range(1, 4):
-        for g in (1, 0):
+            mine, theirs = share(1, 0, 0, p)
+            mine[...] += theirs[...]
+        start(g_sum, k_last, part.at[core, z, 1 - xl], last, lo_dev)
+
+    def fourth():
+        s_col.finish()
+        terms(sr, sc, 4, 1)
+        f_ref[...] = value()
+
+    def next_state():
+        arrived(k_last, last)
+        n_ref[...] = q_ref[...] + last[...]
+        for p in range(PARTS):
+            here = piece(n_ref, p)
+            here[...] = added(here[...], 0, 0, 0, p)
+            for g in (1, 0):
+                for d in (0, 1):
+                    e = (g, d, hops(short, g, d, p), p)
+                    arrived(kr[e], run.at[runs.index(e)])
+                    here[...] += run[runs.index(e)]
+
+    def rows_done():
+        s_row.finish()
+        s_row.from_mate()
+
+    todo = {
+        "begin": begin,
+        "square": square,
+        "product": product,
+        "parts": parts,
+        "sums": sums,
+        "fourth": fourth,
+        "next": next_state,
+        "rows": rows_done,
+        "xe": x_col.exchange,
+        "xl": x_col.launch,
+        "cl": s_col.launch,
+        "xn": lambda: near(ar, xc),
+        "cn": lambda: near(sr, sc),
+    }
+    panels = {"a": (a_col, a_row), "x": (x_col,), "r": (s_row,), "c": (s_col,)}
+
+    def advance(pairs):
+        for g in (0, 1):
             for p in range(PARTS):
-                s_col.step(back, 1 - g, p)
-                for d in (0, 1):
-                    relay(g, d, p, hops(short, g, d, p) - back)
-        if back == 2:
-            s_row.finish()
-            s_row.from_mate()
-    clear()
-    terms(sr, sc, -3, 7)
-    step(4, s_col)
-    s_col.finish()
-    terms(sr, sc, 4, 1)
-    f_ref[...] = value()
-    arrived(k_last, last)
-    n_ref[...] = q_ref[...] + last[...]
-    for p in range(PARTS):
-        here = piece(n_ref, p)
-        here[...] = added(here[...], 0, 0, 0, p)
-        for g in (1, 0):
-            for d in (0, 1):
-                e = (g, d, hops(short, g, d, p), p)
-                arrived(kr[e], run.at[runs.index(e)])
-                here[...] += run[runs.index(e)]
+                for who, i in pairs:
+                    for panel in panels.get(who, ()):
+                        panel.step(i, g, p)
+                    for d in (0, 1) if who == "b" else ():
+                        relay(1 - g, d, p, hops(short, 1 - g, d, p) - i)
+
+    for name in ORDER:
+        if name in todo:
+            todo.pop(name)()
+        else:
+            advance([(name[j], int(name[j + 1])) for j in range(0, len(name), 2)])
     for panel in (a_row, a_col, x_col, s_row, s_col):
         panel.all_sent()
     all_sent(g_part, swap.at[...])
     all_sent(g_sum, ar.at[pl.ds(0, 15)])
+    assert not todo
     assert next(ids) == copies()
 
 
 def on_device(operator, state, source):
-    block = jax.ShapeDtypeStruct((B, H), F32)
+    block = pltpu.VMEM((B, H), F32)
     vmem = pl.BlockSpec(memory_space=pltpu.VMEM)
 
     def blocks(*lead):

time: 96.7 us -> 93.8 us (0.970)
  Pallas kernels: 93.6 us -> 91.7 us
    pallas_call x1, Pallas kernels: 93.6 us -> 91.7 us  [on_device(): pl.pallas_call(kernel, out_shape=(block, block), in_specs=[vmem] * 3, out...]
    unnamed x4 -> x2, local copies, waits for them, and re-layouts: 2.26 us -> 1.31 us
where the time goes in v3:
time: 93.8 us; the launch traced here: 93.6 us
  Pallas kernels  91.7 us (98%)
  local copies, waits for them, and re-layouts  1.31 us (1%)
    pallas_call x1, Pallas kernels, on_device(): pl.pallas_call(kernel, out_shape=(block, block), in_specs=[vmem] * 3, out...  91.7 us

profile of v3, /device:TPU:1, one launch (start us, length us, event | category | flops | bytes accessed | tf_op | source)
XLA Modules:
  0.0 93.6 jit_solution(17595751764805870212)
XLA Ops:
  0.6 91.7 %smith.1 = (f32[256,128]{1,0:T(8,128)S(1)}, f32[256,128]{1,0:T(8,128)S(1)}) custom-call(f32[256,128]{1,0:T(8,128)} %a_ref.1, f32[256,128]{1,0:T(8,128)} %x_ref.1, f32[256,128]{1,0:T(8,128)} %q_ref.1), custom_call_target="tpu_custom_call" | custom-call | tf_op jit(solution)/shard_map/smith/pallas_call | solution.py:413
  92.3 0.7 copy.7
  93.0 0.7 copy.8
